TPU v7x, 32 devices: a whole 2x2x4 slice. The times are simulated.
32 devices in a mesh: grp: 4 (over y, x), mem: 8 (over z, core).
Axes of the slice: x: 2, y: 2, z: 4, core: 2. Of those that a mesh axis runs over, the one named last changes fastest.
Arguments:
- factors: bfloat16 [32, 512, 2048], P(('grp', 'mem')), may hold values from -1 to 1
- occ_energy: bfloat16 [32], P(('grp', 'mem')), may hold values from -1.5 to -0.29882812
- vir_energy: bfloat16 [512], replicated, may hold values from 0.3984375 to 3
- pair_code: int32 [4, 8, 3], P('grp'), may hold values from 0 to 2
- pair_count: int32 [4, 8], P('grp'), may hold values from 1 to 3
Outputs:
- aux_density: bfloat16 [32, 512, 2048], P(('grp', 'mem'))
- lagrangian: bfloat16 [32, 512, 2048], P(('grp', 'mem'))
Inputs may be any that keep to these rules, and one draw needn't show every extreme that they name: `pair_code`: only the first pair_count entries of a device's list are read; entries may repeat.
All inputs are finite; a program needn't handle non-finite values.
Results may differ from a plain program's by a relative error of at most 0.0056.
Values may be sent and summed in bfloat16 or wider, within the bound.
No kernel may reach another device: no remote copies, remote signals or barrier semaphores. Data moves between devices by JAX's collectives and lax.ppermute only.
A program may use at most 128 MiB of HBM per device.

v0:
```python
import jax
import jax.numpy as jnp
from jax import lax
from jax.sharding import PartitionSpec as P

OCC_DEV = 1
ROUNDS = 2


def partner(value, axis, distance):
    mask = 2**distance
    pairs = [(source, source ^ mask) for source in range(lax.axis_size(axis))]
    return lax.ppermute(value, axis, pairs)


def decode_pair(code):
    round_no = code // (OCC_DEV * OCC_DEV)
    left_orb = code // OCC_DEV % OCC_DEV
    right_orb = code % OCC_DEV
    return (round_no, left_orb, right_orb)


def add_at(target, indices, contribution):
    zero_index = jnp.zeros((), jnp.int32)
    anchor = tuple(indices) + (zero_index,) * contribution.ndim
    extent = (1,) * len(indices) + contribution.shape
    current = lax.dynamic_slice(target, anchor, extent)
    return lax.dynamic_update_slice(target, current + contribution.reshape(extent), anchor)


def outer_terms(amp_tile):
    return lax.dot_general(
        amp_tile, amp_tile, (((1,), (1,)), ((), ())), preferred_element_type=jnp.float32
    )


def near_product(amp_tile, right_block):
    return jnp.dot(amp_tile, right_block, preferred_element_type=jnp.float32)


def far_product(amp_tile, left_block):
    return lax.dot_general(
        amp_tile, left_block, (((0,), (0,)), ((), ())), preferred_element_type=jnp.float32
    )


def per_device(factors, occ_energy, vir_energy, pair_code, pair_count):
    virtual = vir_energy.astype(jnp.float32)
    my_place = lax.axis_index("mem")
    group_codes = pair_code[0]
    group_counts = pair_count[0]
    my_codes = lax.dynamic_index_in_dim(group_codes, my_place, 0, keepdims=False)
    live_count = lax.dynamic_index_in_dim(group_counts, my_place, 0, keepdims=False)
    blocks_all = [factors]
    energy_list = [occ_energy]
    for round_idx in range(ROUNDS):
        visitor, visitor_energy = partner((factors, occ_energy), "mem", round_idx)
        blocks_all.append(visitor)
        energy_list.append(visitor_energy)
    stacked = jnp.stack(blocks_all)
    energy_all = jnp.stack(energy_list).astype(jnp.float32)
    vir_count = factors.shape[1]
    density_zero = jnp.zeros((vir_count, vir_count), jnp.float32)

    def pair_terms(slot_no):
        round_no, left_orb, right_orb = decode_pair(my_codes[slot_no])
        left_block = stacked[0, left_orb]
        right_block = stacked[round_no, right_orb]
        integrals = lax.dot_general(
            left_block, right_block, (((1,), (1,)), ((), ())), preferred_element_type=jnp.float32
        )
        denominator = (
            virtual[:, None]
            + virtual[None, :]
            - energy_all[0, left_orb]
            - energy_all[round_no, right_orb]
        )
        amp_tile = (integrals / denominator).astype(jnp.bfloat16)
        return (round_no, left_orb, right_orb, left_block, right_block, amp_tile)

    def pair_step(slot_no, carry_pair):
        density, totals = carry_pair
        round_no, left_orb, right_orb, left_block, right_block, amp_tile = pair_terms(slot_no)
        density = density + outer_terms(amp_tile)
        totals = add_at(
            totals, (jnp.zeros((), jnp.int32), left_orb), near_product(amp_tile, right_block)
        )
        totals = add_at(totals, (round_no, right_orb), far_product(amp_tile, left_block))
        return (density, totals)

    totals_zero = jnp.zeros((ROUNDS + 1,) + factors.shape, jnp.float32)
    density, totals = lax.fori_loop(0, live_count, pair_step, (density_zero, totals_zero))
    gathered = totals[0]
    for round_idx in range(ROUNDS):
        gathered = gathered + partner(totals[round_idx + 1], "mem", round_idx)
    density = lax.psum(density, "mem")
    density = lax.psum(density, "grp")
    density_scale = 1.0 / (8.0 * lax.axis_size("grp") * lax.axis_size("mem"))
    density_tile = (density * density_scale).astype(jnp.bfloat16)
    lagrangian = jnp.einsum(
        "ab,kbp->kap", density_tile, factors, preferred_element_type=jnp.float32
    )
    return (gathered.astype(jnp.bfloat16), lagrangian.astype(jnp.bfloat16))


def solution(mesh):
    in_specs = (
        P(("grp", "mem"), None, None),
        P(("grp", "mem")),
        P(),
        P("grp", None, None),
        P("grp", None),
    )
    out_specs = (P(("grp", "mem"), None, None), P(("grp", "mem"), None, None))
    return jax.shard_map(
        per_device, mesh=mesh, in_specs=in_specs, out_specs=out_specs, check_vma=False
    )
```

profile of v0, /device:TPU:0, one launch (start us, length us, event | category | flops | bytes accessed | tf_op | source)
XLA Modules:
  0.0 274.6 jit_solution(6055429350554140018)
XLA Ops:
  7.2 0.6 collective-permute-start
  7.8 2.6 collective-permute-start.1
  11.3 0.7 convert_element_type.38
  11.9 1.2 constant_dynamic-slice_fusion.1
  13.4 43.7 %collective-permute-done.3 = bf16[1]{0:T(256)(128)(2,1)} collective-permute-done((bf16[1]{0:T(256)(128)(2,1)}, bf16[1]{0:T(256)(128)(2,1)}, u32[]{:S(2)}, u32[]{:S(2)}) %collective-permute-start.3) | collective-permute-done | bytes 34 | tf_op jit(solution)/shard_map/ppermute | solution.py:13
  57.1 1.3 maximum_convert_fusion
  58.3 5.5 %pad_maximum_fusion = bf16[3,1,512,2048]{3,2,1,0:T(8,128)(2,1)} fusion(bf16[1,1,512,2048]{3,2,1,0:T(8,128)(2,1)} %bitcast.11, bf16[1,1,512,2048]{3,2,1,0:T(8,128)(2,1)S(1)} %bitcast.93, bf16[1,1,512,2048]{3,2,1,0:T(8,128)(2,1)} %bitcast.92), kind=kLoop, calls=%fused_computation.19 | loop fusion | flops 6291456 | bytes 12582912 | tf_op jit(solution)/shard_map/stack | solution.py:60
  63.9 6.1 %broadcast_in_dim.9 = f32[3,1,512,2048]{3,2,1,0:T(8,128)} broadcast(f32[]{:T(128)} %constant.74.clone.1), dimensions={} | broadcast | bytes 12582916 | tf_op jit(solution)/shard_map/broadcast_in_dim | solution.py:91
  70.1 39.3 %while.14 = (s32[]{:T(128)}, f32[512,512]{1,0:T(8,128)S(1)}, f32[3,1,512,2048]{3,2,1,0:T(8,128)}, s32[]{:T(128)}, s32[3]{0:T(128)S(1)}, /*index=5*/bf16[3,1,512,...) while((s32[]{:T(128)}, f32[512,512]{1,0:T(8,128)S(1)}, ...), condition=%wide.region_1.2_spmd, body=%wide.region_0.1_spmd.sunk | while | flops 3493330944 | bytes 155194704 | solution.py:92
  70.7 0.6 dynamic_slice.94
  73.4 0.6 fusion.52
  74.0 6.0 %divide_convert_fusion.2 = bf16[512,512]{0,1:T(8,128)(2,1)S(1)} fusion(bf16[3,1,512,2048]{3,2,1,0:T(8,128)(2,1)} %get-tuple-element.212, s32[]{:T(128)S(6)} %select_n.46, f32[]{:T(128)} %bitcast.89, f32[]{:T(128)} %bitcast.90, f32[512]{0:T(512)S(1)} %get-tuple-element.213), kind=kOutput, calls=%fused_computation.15.clone.1 | convolution fusion | flops 1075052544 | bytes 4723716 | tf_op jit(solution)/shard_map/while/body/dot_general | solution.py:69
  80.0 0.5 convolution_add_fusion.2
  80.5 1.1 copy-done.3
  81.7 1.6 fusion.53
  83.2 1.6 fusion.54
  84.9 4.5 %copy-done.2 = f32[3,1,512,2048]{3,2,1,0:T(8,128)} copy-done((f32[3,1,512,2048]{3,2,1,0:T(8,128)}, f32[3,1,512,2048]{3,2,1,0:T(8,128)S(1)}, u32[]{:S(2)}) %copy-start.2) | copy-done | bytes 12582936 | tf_op jit(solution)/shard_map/while
  90.1 0.6 dynamic_slice.94
  92.7 0.6 fusion.52
  93.4 6.0 %divide_convert_fusion.2 = bf16[512,512]{0,1:T(8,128)(2,1)S(1)} fusion(bf16[3,1,512,2048]{3,2,1,0:T(8,128)(2,1)} %get-tuple-element.212, s32[]{:T(128)S(6)} %select_n.46, f32[]{:T(128)} %bitcast.89, f32[]{:T(128)} %bitcast.90, f32[512]{0:T(512)S(1)} %get-tuple-element.213), kind=kOutput, calls=%fused_computation.15.clone.1 | convolution fusion | flops 1075052544 | bytes 4723716 | tf_op jit(solution)/shard_map/while/body/dot_general | solution.py:69
  99.4 0.5 convolution_add_fusion.2
  99.9 1.1 copy-done.3
  101.0 1.6 fusion.53
  102.6 1.6 fusion.54
  104.2 4.5 %copy-done.2 = f32[3,1,512,2048]{3,2,1,0:T(8,128)} copy-done((f32[3,1,512,2048]{3,2,1,0:T(8,128)}, f32[3,1,512,2048]{3,2,1,0:T(8,128)S(1)}, u32[]{:S(2)}) %copy-start.2) | copy-done | bytes 12582936 | tf_op jit(solution)/shard_map/while
  109.4 8.2 %slice_bitcast_fusion.1 = (f32[1,512,2048]{2,1,0:T(8,128)}, f32[1,512,2048]{2,1,0:T(8,128)}) fusion(f32[3,1,512,2048]{3,2,1,0:T(8,128)} %get-tuple-element.109), kind=kLoop, calls=%fused_computation.24 | loop fusion | bytes 16777216 | tf_op jit(solution)/shard_map/squeeze | solution.py:95
  117.7 19.1 %collective-permute-start.4 = (f32[1,512,2048]{2,1,0:T(8,128)}, f32[1,512,2048]{2,1,0:T(8,128)}, u32[]{:S(2)}, u32[]{:S(2)}) collective-permute-start(f32[1,512,2048]{2,1,0:T(8,128)} %get-tuple-element.129), channel_id=1, source_target_pairs={{0,1},{1,0},{2,3},{3,2},{4,5},{5,4},{6,7},{7,6},{8,9},{9,8},{10,11... | collective-permute-start | bytes 12582920 | tf_op jit(solution)/shard_map/ppermute | solution.py:13
  136.8 2.0 collective-permute-start.5
  138.8 63.4 %all-reduce.3.cloned.1.call-done = f32[512,512]{1,0:T(8,128)} async-done(((f32[512,512]{1,0:T(8,128)}), f32[512,512]{1,0:T(8,128)}) %all-reduce.3.cloned.1.call-update) | async-done | bytes 1048592 | tf_op jit(solution)/shard_map/psum | solution.py:96
  202.3 54.6 %all-reduce.5.cloned.1.call-done = f32[512,512]{1,0:T(8,128)} async-done(((f32[512,512]{1,0:T(8,128)}), f32[512,512]{1,0:T(8,128)}) %all-reduce.5.cloned.1.call-update) | async-done | bytes 1048592 | tf_op jit(solution)/shard_map/psum | solution.py:97
  256.9 3.8 %fusion.24 = bf16[1,512,2048]{2,1,0:T(8,128)(2,1)} fusion(bf16[1,512,2048]{2,1,0:T(8,128)(2,1)S(1)} %copy-done.5, f32[512,512]{1,0:T(8,128)} %all-reduce.5.cloned.1.call-done), kind=kOutput, calls=%fused_computation.26 | convolution fusion | flops 1075314688 | bytes 5242880 | tf_op jit(solution)/shard_map/ab,kbp->kap/dot_general | solution.py:100
  260.7 7.1 %fusion.23 = bf16[1,512,2048]{2,1,0:T(8,128)(2,1)} fusion(f32[1,512,2048]{2,1,0:T(8,128)} %collective-permute-done.5, f32[1,512,2048]{2,1,0:T(8,128)} %collective-permute-done.4, f32[3,1,512,2048]{3,2,1,0:T(8,128)} %get-tuple-element.109), kind=kLoop, calls=%fused_computation.22 | loop fusion | flops 3145728 | bytes 14680064 | tf_op jit(solution)/shard_map/convert_element_type | solution.py:103
  (27 shorter events, 0.7 us)
Async XLA Ops:
  7.2 6.0 %copy-start = (s32[1,8,3]{1,0,2:T(1,128)S(1)}, s32[1,8,3]{1,0,2:T(1,128)}, u32[]{:S(2)}) copy-start(s32[1,8,3]{1,0,2:T(1,128)} %param.10) | copy-start | bytes 292
  7.2 195.1 %all-reduce.3.cloned.1.call-start = ((), (), s32[]{:S(2)}) async-start(), calls=%async_computation | async-start | bytes 2097152 | tf_op jit(solution)/shard_map/psum | solution.py:96
  7.2 51.1 %collective-permute-start = (bf16[1,512,2048]{2,1,0:T(8,128)(2,1)}, bf16[1,512,2048]{2,1,0:T(8,128)(2,1)S(1)}, u32[]{:S(2)}, u32[]{:S(2)}) collective-permute-start(bf16[1,512,2048]{2,1,0:T(8,128)(2,1)} %param.7), channel_id=1, source_target_pairs={{0,1},{1,0},{2,3},{3,2},{4,5},{5,4},{6,7},{7,6},{8,9},{9,8},{10,11... | collective-permute-start | bytes 6291464 | tf_op jit(solution)/shard_map/ppermute | solution.py:13
  7.8 50.5 %collective-permute-start.1 = (bf16[1,512,2048]{2,1,0:T(8,128)(2,1)}, bf16[1,512,2048]{2,1,0:T(8,128)(2,1)}, u32[]{:S(2)}, u32[]{:S(2)}) collective-permute-start(bf16[1,512,2048]{2,1,0:T(8,128)(2,1)} %param.7), channel_id=1, source_target_pairs={{0,2},{1,3},{2,0},{3,1},{4,6},{5,7},{6,4},{7,5},{8,10},{9,11},{10,... | collective-permute-start | bytes 6291464 | tf_op jit(solution)/shard_map/ppermute | solution.py:13
  10.4 46.6 %collective-permute-start.3 = (bf16[1]{0:T(256)(128)(2,1)}, bf16[1]{0:T(256)(128)(2,1)}, u32[]{:S(2)}, u32[]{:S(2)}) collective-permute-start(bf16[1]{0:T(256)(128)(2,1)} %param.8), channel_id=1, source_target_pairs={{0,2},{1,3},{2,0},{3,1},{4,6},{5,7},{6,4},{7,5},{8,10},{9,11},{10,... | collective-permute-start | bytes 14 | tf_op jit(solution)/shard_map/ppermute | solution.py:13
  10.5 46.6 %collective-permute-start.2 = (bf16[1]{0:T(256)(128)(2,1)}, bf16[1]{0:T(256)(128)(2,1)}, u32[]{:S(2)}, u32[]{:S(2)}) collective-permute-start(bf16[1]{0:T(256)(128)(2,1)} %param.8), channel_id=1, source_target_pairs={{0,1},{1,0},{2,3},{3,2},{4,5},{5,4},{6,7},{7,6},{8,9},{9,8},{10,11... | collective-permute-start | bytes 14 | tf_op jit(solution)/shard_map/ppermute | solution.py:13
  74.0 6.5 %copy-start.1 = (f32[3,1,512,2048]{3,2,1,0:T(8,128)S(1)}, f32[3,1,512,2048]{3,2,1,0:T(8,128)}, u32[]{:S(2)}) copy-start(f32[3,1,512,2048]{3,2,1,0:T(8,128)} %get-tuple-element.198) | copy-start | bytes 37748740 | tf_op jit(solution)/shard_map/while
  74.0 7.6 %copy-start.3 = (bf16[3,1,512,2048]{3,2,1,0:T(8,128)(2,1)S(1)}, bf16[3,1,512,2048]{3,2,1,0:T(8,128)(2,1)}, u32[]{:S(2)}) copy-start(bf16[3,1,512,2048]{3,2,1,0:T(8,128)(2,1)} %get-tuple-element.212) | copy-start | bytes 18874372 | tf_op jit(solution)/shard_map/while
  84.9 4.5 %copy-start.2 = (f32[3,1,512,2048]{3,2,1,0:T(8,128)}, f32[3,1,512,2048]{3,2,1,0:T(8,128)S(1)}, u32[]{:S(2)}) copy-start(f32[3,1,512,2048]{3,2,1,0:T(8,128)S(1)} %fusion.54) | copy-start | bytes 37748740 | tf_op jit(solution)/shard_map/while
  93.4 6.5 %copy-start.1 = (f32[3,1,512,2048]{3,2,1,0:T(8,128)S(1)}, f32[3,1,512,2048]{3,2,1,0:T(8,128)}, u32[]{:S(2)}) copy-start(f32[3,1,512,2048]{3,2,1,0:T(8,128)} %get-tuple-element.198) | copy-start | bytes 37748740 | tf_op jit(solution)/shard_map/while
  93.4 7.6 %copy-start.3 = (bf16[3,1,512,2048]{3,2,1,0:T(8,128)(2,1)S(1)}, bf16[3,1,512,2048]{3,2,1,0:T(8,128)(2,1)}, u32[]{:S(2)}) copy-start(bf16[3,1,512,2048]{3,2,1,0:T(8,128)(2,1)} %get-tuple-element.212) | copy-start | bytes 18874372 | tf_op jit(solution)/shard_map/while
  104.2 4.5 %copy-start.2 = (f32[3,1,512,2048]{3,2,1,0:T(8,128)}, f32[3,1,512,2048]{3,2,1,0:T(8,128)S(1)}, u32[]{:S(2)}) copy-start(f32[3,1,512,2048]{3,2,1,0:T(8,128)S(1)} %fusion.54) | copy-start | bytes 37748740 | tf_op jit(solution)/shard_map/while
  109.4 8.3 %copy-start.4 = (f32[512,512]{1,0:T(8,128)}, f32[512,512]{1,0:T(8,128)S(1)}, u32[]{:S(2)}) copy-start(f32[512,512]{1,0:T(8,128)S(1)} %get-tuple-element.110) | copy-start | bytes 3145732
  109.4 147.5 %copy-start.5 = (bf16[1,512,2048]{2,1,0:T(8,128)(2,1)S(1)}, bf16[1,512,2048]{2,1,0:T(8,128)(2,1)}, u32[]{:S(2)}) copy-start(bf16[1,512,2048]{2,1,0:T(8,128)(2,1)} %param.7) | copy-start | bytes 6291460
  117.7 143.0 %collective-permute-start.4 = (f32[1,512,2048]{2,1,0:T(8,128)}, f32[1,512,2048]{2,1,0:T(8,128)}, u32[]{:S(2)}, u32[]{:S(2)}) collective-permute-start(f32[1,512,2048]{2,1,0:T(8,128)} %get-tuple-element.129), channel_id=1, source_target_pairs={{0,1},{1,0},{2,3},{3,2},{4,5},{5,4},{6,7},{7,6},{8,9},{9,8},{10,11... | collective-permute-start | bytes 12582920 | tf_op jit(solution)/shard_map/ppermute | solution.py:13
  136.8 123.9 %collective-permute-start.5 = (f32[1,512,2048]{2,1,0:T(8,128)}, f32[1,512,2048]{2,1,0:T(8,128)}, u32[]{:S(2)}, u32[]{:S(2)}) collective-permute-start(f32[1,512,2048]{2,1,0:T(8,128)} %get-tuple-element.130), channel_id=1, source_target_pairs={{0,2},{1,3},{2,0},{3,1},{4,6},{5,7},{6,4},{7,5},{8,10},{9,11},{10,... | collective-permute-start | bytes 12582920 | tf_op jit(solution)/shard_map/ppermute | solution.py:13
  138.8 118.1 %all-reduce.5.cloned.1.call-start = ((), (), s32[]{:S(2)}) async-start(), calls=%async_computation.1 | async-start | bytes 2097152 | tf_op jit(solution)/shard_map/psum | solution.py:97
Sparse Core Ops, SparseCore 0:
  138.9 63.3 all-reduce.2
  205.3 51.5 all-reduce.4
where the time goes:
time: 275 us
  waiting for transfers between devices  162 us (59%)
  local copies, waits for them, and re-layouts  29.9 us (11%)
  starting transfers between devices  24.5 us (9%)
  matrix products  23.1 us (8%)
  between operations  14.7 us (5%)
  other arithmetic  14.5 us (5%)
  loops' own time  6.11 us (2%)
    psum x1, waiting for transfers between devices, per_device(): density = lax.psum(density, 'mem')  63.4 us
    psum x1, waiting for transfers between devices, per_device(): density = lax.psum(density, 'grp')  54.6 us
    ppermute x6, waiting for transfers between devices, partner(): return lax.ppermute(value, axis, pairs)  43.7 us
    ppermute x6, starting transfers between devices, partner(): return lax.ppermute(value, axis, pairs)  24.4 us
    dot_general x2, matrix products, pair_terms(): lax.dot_general(left_block, right_block, (((1,), (1,)), ((), ())), prefer...  12 us
    while x12, local copies, waits for them, and re-layouts  11.3 us
    squeeze x1, local copies, waits for them, and re-layouts, per_device(): gathered = gathered + partner(totals[round_idx + 1], 'mem', round_idx)  8.24 us
    convert_element_type x1, other arithmetic, per_device(): return (gathered.astype(jnp.bfloat16), lagrangian.astype(jnp.bfloat16))  7.07 us
  transfers between devices with their start and end apart: 8, of which 3 were waited for; matrix products, arithmetic and copies ran while one was open for 3% of the time, Pallas kernels for 0%

commit v1 on v0

--- a/solution.py
+++ b/solution.py
@@ -1,3 +1,4 @@
+import functools
 import jax
 import jax.numpy as jnp
 from jax import lax
@@ -5,6 +6,21 @@
 
 OCC_DEV = 1
 ROUNDS = 2
+
+
+def _match_lanes(local_values, bus_axis):
+    n_shards = lax.axis_size(bus_axis)
+    x_next = local_values
+    for src_i in [idx for idx in (1, 2, 4, 8, 16) if idx < n_shards]:
+        back = range(n_shards)
+        all_values = map(lambda dev_i: (dev_i, dev_i ^ src_i), back)
+        state_next = list(all_values)
+        long_array = lax.ppermute(x_next, bus_axis, state_next)
+        x_next = x_next + long_array
+    return x_next
+
+
+render_scenes = functools.partial(_match_lanes, bus_axis="mem")
 
 
 def partner(value, axis, distance):
@@ -93,7 +109,7 @@
     gathered = totals[0]
     for round_idx in range(ROUNDS):
         gathered = gathered + partner(totals[round_idx + 1], "mem", round_idx)
-    density = lax.psum(density, "mem")
+    density = render_scenes(density)
     density = lax.psum(density, "grp")
     density_scale = 1.0 / (8.0 * lax.axis_size("grp") * lax.axis_size("mem"))
     density_tile = (density * density_scale).astype(jnp.bfloat16)

time: 275 us -> 365 us (1.33)
  waiting for transfers between devices: 162 us -> 249 us
    ppermute x0 -> x3, waiting for transfers between devices: none -> 159 us  [_match_lanes(): long_array = lax.ppermute(x_next, bus_axis, state_next)]
    psum x1 -> x0, waiting for transfers between devices: 63.4 us -> none  [per_device(): density = lax.psum(density, 'mem')]
    psum x1, waiting for transfers between devices: 54.6 us -> 45.7 us  [per_device(): density = lax.psum(density, 'grp')]
  transfers between devices with their start and end apart: 8 -> 10, of which waited for: 3 -> 5; matrix products, arithmetic and copies ran while one was open for 3% -> 3% of each run, Pallas kernels for 0% -> 0%
where the time goes in v1:
time: 365 us
  waiting for transfers between devices  249 us (68%)
  local copies, waits for them, and re-layouts  29.4 us (8%)
  starting transfers between devices  26.9 us (7%)
  matrix products  23 us (6%)
  other arithmetic  16.2 us (4%)
  between operations  14.8 us (4%)
  loops' own time  5.83 us (2%)
    ppermute x3, waiting for transfers between devices, _match_lanes(): long_array = lax.ppermute(x_next, bus_axis, state_next)  159 us
    psum x1, waiting for transfers between devices, per_device(): density = lax.psum(density, 'grp')  45.7 us
    ppermute x6, waiting for transfers between devices, partner(): return lax.ppermute(value, axis, pairs)  43.6 us
    ppermute x6, starting transfers between devices, partner(): return lax.ppermute(value, axis, pairs)  24.2 us
    dot_general x2, matrix products, pair_terms(): lax.dot_general(left_block, right_block, (((1,), (1,)), ((), ())), prefer...  11.9 us
    while x12, local copies, waits for them, and re-layouts  11.5 us
    squeeze x1, local copies, waits for them, and re-layouts, per_device(): gathered = gathered + partner(totals[round_idx + 1], 'mem', round_idx)  7.86 us
  transfers between devices with their start and end apart: 10, of which 5 were waited for; matrix products, arithmetic and copies ran while one was open for 3% of the time, Pallas kernels for 0%

profile of v1, /device:TPU:0, one launch (start us, length us, event | category | flops | bytes accessed | tf_op | source)
XLA Modules:
  0.0 364.8 jit_solution(5782406197727666720)
XLA Ops:
  7.8 2.6 collective-permute-start.1
  11.3 0.7 convert_element_type.38
  11.9 1.2 constant_dynamic-slice_fusion.1
  13.4 43.6 %collective-permute-done.3 = bf16[1]{0:T(256)(128)(2,1)} collective-permute-done((bf16[1]{0:T(256)(128)(2,1)}, bf16[1]{0:T(256)(128)(2,1)}, u32[]{:S(2)}, u32[]{:S(2)}) %collective-permute-start.3) | collective-permute-done | bytes 34 | tf_op jit(solution)/shard_map/ppermute | solution.py:29
  57.0 1.2 maximum_convert_fusion
  58.2 5.5 %pad_maximum_fusion = bf16[3,1,512,2048]{3,2,1,0:T(8,128)(2,1)} fusion(bf16[1,1,512,2048]{3,2,1,0:T(8,128)(2,1)} %bitcast.11, bf16[1,1,512,2048]{3,2,1,0:T(8,128)(2,1)S(1)} %bitcast.93, bf16[1,1,512,2048]{3,2,1,0:T(8,128)(2,1)} %bitcast.92), kind=kLoop, calls=%fused_computation.19 | loop fusion | flops 6291456 | bytes 12582912 | tf_op jit(solution)/shard_map/stack | solution.py:76
  63.8 6.1 %broadcast_in_dim.9 = f32[3,1,512,2048]{3,2,1,0:T(8,128)} broadcast(f32[]{:T(128)} %constant.74.clone.1), dimensions={} | broadcast | bytes 12582916 | tf_op jit(solution)/shard_map/broadcast_in_dim | solution.py:107
  69.9 38.9 %while.14 = (s32[]{:T(128)}, f32[512,512]{1,0:T(8,128)S(1)}, f32[3,1,512,2048]{3,2,1,0:T(8,128)}, s32[]{:T(128)}, s32[3]{0:T(128)S(1)}, /*index=5*/bf16[3,1,512,...) while((s32[]{:T(128)}, f32[512,512]{1,0:T(8,128)S(1)}, ...), condition=%wide.region_1.2_spmd, body=%wide.region_0.1_spmd.sunk | while | flops 3493330944 | bytes 155194704 | solution.py:108
  70.6 0.6 dynamic_slice.94
  73.1 0.6 fusion.52
  73.7 5.9 %divide_convert_fusion.2 = bf16[512,512]{0,1:T(8,128)(2,1)S(1)} fusion(bf16[3,1,512,2048]{3,2,1,0:T(8,128)(2,1)} %get-tuple-element.212, s32[]{:T(128)S(6)} %select_n.46, f32[]{:T(128)} %bitcast.89, f32[]{:T(128)} %bitcast.90, f32[512]{0:T(512)S(1)} %get-tuple-element.213), kind=kOutput, calls=%fused_computation.15.clone.1 | convolution fusion | flops 1075052544 | bytes 4723716 | tf_op jit(solution)/shard_map/while/body/dot_general | solution.py:85
  80.1 1.2 copy-done.3
  81.3 1.6 fusion.53
  82.9 1.6 fusion.54
  84.5 4.5 %copy-done.2 = f32[3,1,512,2048]{3,2,1,0:T(8,128)} copy-done((f32[3,1,512,2048]{3,2,1,0:T(8,128)}, f32[3,1,512,2048]{3,2,1,0:T(8,128)S(1)}, u32[]{:S(2)}) %copy-start.2) | copy-done | bytes 12582936 | tf_op jit(solution)/shard_map/while
  92.2 0.6 fusion.52
  92.8 5.9 %divide_convert_fusion.2 = bf16[512,512]{0,1:T(8,128)(2,1)S(1)} fusion(bf16[3,1,512,2048]{3,2,1,0:T(8,128)(2,1)} %get-tuple-element.212, s32[]{:T(128)S(6)} %select_n.46, f32[]{:T(128)} %bitcast.89, f32[]{:T(128)} %bitcast.90, f32[512]{0:T(512)S(1)} %get-tuple-element.213), kind=kOutput, calls=%fused_computation.15.clone.1 | convolution fusion | flops 1075052544 | bytes 4723716 | tf_op jit(solution)/shard_map/while/body/dot_general | solution.py:85
  99.2 1.2 copy-done.3
  100.4 1.6 fusion.53
  102.0 1.6 fusion.54
  103.6 4.5 %copy-done.2 = f32[3,1,512,2048]{3,2,1,0:T(8,128)} copy-done((f32[3,1,512,2048]{3,2,1,0:T(8,128)}, f32[3,1,512,2048]{3,2,1,0:T(8,128)S(1)}, u32[]{:S(2)}) %copy-start.2) | copy-done | bytes 12582936 | tf_op jit(solution)/shard_map/while
  108.8 7.9 %slice_bitcast_fusion.1 = (f32[1,512,2048]{2,1,0:T(8,128)}, f32[1,512,2048]{2,1,0:T(8,128)}) fusion(f32[3,1,512,2048]{3,2,1,0:T(8,128)} %get-tuple-element.109), kind=kLoop, calls=%fused_computation.24 | loop fusion | bytes 16777216 | tf_op jit(solution)/shard_map/squeeze | solution.py:111
  116.7 19.0 %collective-permute-start.4 = (f32[1,512,2048]{2,1,0:T(8,128)}, f32[1,512,2048]{2,1,0:T(8,128)}, u32[]{:S(2)}, u32[]{:S(2)}) collective-permute-start(f32[1,512,2048]{2,1,0:T(8,128)} %get-tuple-element.129), channel_id=1, source_target_pairs={{0,1},{1,0},{2,3},{3,2},{4,5},{5,4},{6,7},{7,6},{8,9},{9,8},{10,11... | collective-permute-start | bytes 12582920 | tf_op jit(solution)/shard_map/ppermute | solution.py:29
  135.6 1.9 collective-permute-start.5
  137.8 6.4 %collective-permute-done.6 = f32[512,512]{1,0:T(8,128)S(1)} collective-permute-done((f32[512,512]{1,0:T(8,128)S(1)}, f32[512,512]{1,0:T(8,128)S(1)}, u32[]{:S(2)}, u32[]{:S(2)}) %collective-permute-start.6) | collective-permute-done | bytes 1048608 | tf_op jit(solution)/shard_map/ppermute | solution.py:18
  144.3 2.3 collective-permute-start.7
  146.7 104.8 %collective-permute-done.7 = f32[512,512]{1,0:T(8,128)S(1)} collective-permute-done((f32[512,512]{1,0:T(8,128)S(1)}, f32[512,512]{1,0:T(8,128)S(1)}, u32[]{:S(2)}, u32[]{:S(2)}) %collective-permute-start.7) | collective-permute-done | bytes 1048608 | tf_op jit(solution)/shard_map/ppermute | solution.py:18
  251.7 48.2 %collective-permute-done.8 = f32[512,512]{1,0:T(8,128)S(1)} collective-permute-done((f32[512,512]{1,0:T(8,128)S(1)}, f32[512,512]{1,0:T(8,128)S(1)}, u32[]{:S(2)}, u32[]{:S(2)}) %collective-permute-start.8) | collective-permute-done | bytes 1048608 | tf_op jit(solution)/shard_map/ppermute | solution.py:18
  300.0 1.2 add.104
  301.2 7.2 %fusion.23 = bf16[1,512,2048]{2,1,0:T(8,128)(2,1)} fusion(f32[1,512,2048]{2,1,0:T(8,128)} %collective-permute-done.5, f32[1,512,2048]{2,1,0:T(8,128)} %collective-permute-done.4, f32[3,1,512,2048]{3,2,1,0:T(8,128)} %get-tuple-element.109), kind=kLoop, calls=%fused_computation.22 | loop fusion | flops 3145728 | bytes 14680064 | tf_op jit(solution)/shard_map/convert_element_type | solution.py:119
  308.4 45.7 %all-reduce.2.cloned.1.call-done = f32[512,512]{1,0:T(8,128)} async-done(((f32[512,512]{1,0:T(8,128)}), f32[512,512]{1,0:T(8,128)}) %all-reduce.2.cloned.1.call-update) | async-done | bytes 1048592 | tf_op jit(solution)/shard_map/psum | solution.py:113
  354.1 3.8 %fusion.24 = bf16[1,512,2048]{2,1,0:T(8,128)(2,1)} fusion(bf16[1,512,2048]{2,1,0:T(8,128)(2,1)S(1)} %copy-done.4, f32[512,512]{1,0:T(8,128)} %all-reduce.2.cloned.1.call-done), kind=kOutput, calls=%fused_computation.26 | convolution fusion | flops 1075314688 | bytes 5242880 | tf_op jit(solution)/shard_map/ab,kbp->kap/dot_general | solution.py:116
  (31 shorter events, 3.4 us)
Async XLA Ops:
  7.2 6.0 %copy-start = (s32[1,8,3]{1,0,2:T(1,128)S(1)}, s32[1,8,3]{1,0,2:T(1,128)}, u32[]{:S(2)}) copy-start(s32[1,8,3]{1,0,2:T(1,128)} %param.10) | copy-start | bytes 292
  7.2 346.9 %all-reduce.2.cloned.1.call-start = ((), (), s32[]{:S(2)}) async-start(), calls=%async_computation | async-start | bytes 2097152 | tf_op jit(solution)/shard_map/psum | solution.py:113
  7.2 51.0 %collective-permute-start = (bf16[1,512,2048]{2,1,0:T(8,128)(2,1)}, bf16[1,512,2048]{2,1,0:T(8,128)(2,1)S(1)}, u32[]{:S(2)}, u32[]{:S(2)}) collective-permute-start(bf16[1,512,2048]{2,1,0:T(8,128)(2,1)} %param.7), channel_id=1, source_target_pairs={{0,1},{1,0},{2,3},{3,2},{4,5},{5,4},{6,7},{7,6},{8,9},{9,8},{10,11... | collective-permute-start | bytes 6291464 | tf_op jit(solution)/shard_map/ppermute | solution.py:29
  7.8 50.4 %collective-permute-start.1 = (bf16[1,512,2048]{2,1,0:T(8,128)(2,1)}, bf16[1,512,2048]{2,1,0:T(8,128)(2,1)}, u32[]{:S(2)}, u32[]{:S(2)}) collective-permute-start(bf16[1,512,2048]{2,1,0:T(8,128)(2,1)} %param.7), channel_id=1, source_target_pairs={{0,2},{1,3},{2,0},{3,1},{4,6},{5,7},{6,4},{7,5},{8,10},{9,11},{10,... | collective-permute-start | bytes 6291464 | tf_op jit(solution)/shard_map/ppermute | solution.py:29
  10.4 46.5 %collective-permute-start.3 = (bf16[1]{0:T(256)(128)(2,1)}, bf16[1]{0:T(256)(128)(2,1)}, u32[]{:S(2)}, u32[]{:S(2)}) collective-permute-start(bf16[1]{0:T(256)(128)(2,1)} %param.8), channel_id=1, source_target_pairs={{0,2},{1,3},{2,0},{3,1},{4,6},{5,7},{6,4},{7,5},{8,10},{9,11},{10,... | collective-permute-start | bytes 14 | tf_op jit(solution)/shard_map/ppermute | solution.py:29
  10.5 46.5 %collective-permute-start.2 = (bf16[1]{0:T(256)(128)(2,1)}, bf16[1]{0:T(256)(128)(2,1)}, u32[]{:S(2)}, u32[]{:S(2)}) collective-permute-start(bf16[1]{0:T(256)(128)(2,1)} %param.8), channel_id=1, source_target_pairs={{0,1},{1,0},{2,3},{3,2},{4,5},{5,4},{6,7},{7,6},{8,9},{9,8},{10,11... | collective-permute-start | bytes 14 | tf_op jit(solution)/shard_map/ppermute | solution.py:29
  73.7 6.4 %copy-start.1 = (f32[3,1,512,2048]{3,2,1,0:T(8,128)S(1)}, f32[3,1,512,2048]{3,2,1,0:T(8,128)}, u32[]{:S(2)}) copy-start(f32[3,1,512,2048]{3,2,1,0:T(8,128)} %get-tuple-element.198) | copy-start | bytes 37748740 | tf_op jit(solution)/shard_map/while
  73.7 7.6 %copy-start.3 = (bf16[3,1,512,2048]{3,2,1,0:T(8,128)(2,1)S(1)}, bf16[3,1,512,2048]{3,2,1,0:T(8,128)(2,1)}, u32[]{:S(2)}) copy-start(bf16[3,1,512,2048]{3,2,1,0:T(8,128)(2,1)} %get-tuple-element.212) | copy-start | bytes 18874372 | tf_op jit(solution)/shard_map/while
  84.5 4.5 %copy-start.2 = (f32[3,1,512,2048]{3,2,1,0:T(8,128)}, f32[3,1,512,2048]{3,2,1,0:T(8,128)S(1)}, u32[]{:S(2)}) copy-start(f32[3,1,512,2048]{3,2,1,0:T(8,128)S(1)} %fusion.54) | copy-start | bytes 37748740 | tf_op jit(solution)/shard_map/while
  92.8 6.4 %copy-start.1 = (f32[3,1,512,2048]{3,2,1,0:T(8,128)S(1)}, f32[3,1,512,2048]{3,2,1,0:T(8,128)}, u32[]{:S(2)}) copy-start(f32[3,1,512,2048]{3,2,1,0:T(8,128)} %get-tuple-element.198) | copy-start | bytes 37748740 | tf_op jit(solution)/shard_map/while
  92.8 7.6 %copy-start.3 = (bf16[3,1,512,2048]{3,2,1,0:T(8,128)(2,1)S(1)}, bf16[3,1,512,2048]{3,2,1,0:T(8,128)(2,1)}, u32[]{:S(2)}) copy-start(bf16[3,1,512,2048]{3,2,1,0:T(8,128)(2,1)} %get-tuple-element.212) | copy-start | bytes 18874372 | tf_op jit(solution)/shard_map/while
  103.6 4.5 %copy-start.2 = (f32[3,1,512,2048]{3,2,1,0:T(8,128)}, f32[3,1,512,2048]{3,2,1,0:T(8,128)S(1)}, u32[]{:S(2)}) copy-start(f32[3,1,512,2048]{3,2,1,0:T(8,128)S(1)} %fusion.54) | copy-start | bytes 37748740 | tf_op jit(solution)/shard_map/while
  116.7 184.5 %collective-permute-start.4 = (f32[1,512,2048]{2,1,0:T(8,128)}, f32[1,512,2048]{2,1,0:T(8,128)}, u32[]{:S(2)}, u32[]{:S(2)}) collective-permute-start(f32[1,512,2048]{2,1,0:T(8,128)} %get-tuple-element.129), channel_id=1, source_target_pairs={{0,1},{1,0},{2,3},{3,2},{4,5},{5,4},{6,7},{7,6},{8,9},{9,8},{10,11... | collective-permute-start | bytes 12582920 | tf_op jit(solution)/shard_map/ppermute | solution.py:29
  135.6 165.6 %collective-permute-start.5 = (f32[1,512,2048]{2,1,0:T(8,128)}, f32[1,512,2048]{2,1,0:T(8,128)}, u32[]{:S(2)}, u32[]{:S(2)}) collective-permute-start(f32[1,512,2048]{2,1,0:T(8,128)} %get-tuple-element.130), channel_id=1, source_target_pairs={{0,2},{1,3},{2,0},{3,1},{4,6},{5,7},{6,4},{7,5},{8,10},{9,11},{10,... | collective-permute-start | bytes 12582920 | tf_op jit(solution)/shard_map/ppermute | solution.py:29
  137.5 6.6 %collective-permute-start.6 = (f32[512,512]{1,0:T(8,128)S(1)}, f32[512,512]{1,0:T(8,128)S(1)}, u32[]{:S(2)}, u32[]{:S(2)}) collective-permute-start(f32[512,512]{1,0:T(8,128)S(1)} %get-tuple-element.110), channel_id=1, source_target_pairs={{0,1},{1,0},{2,3},{3,2},{4,5},{5,4},{6,7},{7,6},{8,9},{9,8},{10,11... | collective-permute-start | bytes 3145736 | tf_op jit(solution)/shard_map/ppermute | solution.py:18
  144.3 107.1 %collective-permute-start.7 = (f32[512,512]{1,0:T(8,128)S(1)}, f32[512,512]{1,0:T(8,128)S(1)}, u32[]{:S(2)}, u32[]{:S(2)}) collective-permute-start(f32[512,512]{1,0:T(8,128)S(1)} %add.102), channel_id=1, source_target_pairs={{0,2},{1,3},{2,0},{3,1},{4,6},{5,7},{6,4},{7,5},{8,10},{9,11},{10,... | collective-permute-start | bytes 3145736 | tf_op jit(solution)/shard_map/ppermute | solution.py:18
  251.7 48.3 %collective-permute-start.8 = (f32[512,512]{1,0:T(8,128)S(1)}, f32[512,512]{1,0:T(8,128)S(1)}, u32[]{:S(2)}, u32[]{:S(2)}) collective-permute-start(f32[512,512]{1,0:T(8,128)S(1)} %add.103), channel_id=1, source_target_pairs={{0,4},{1,5},{2,6},{3,7},{4,0},{5,1},{6,2},{7,3},{8,12},{9,13},{10,... | collective-permute-start | bytes 3145736 | tf_op jit(solution)/shard_map/ppermute | solution.py:18
  301.2 52.9 %copy-start.4 = (bf16[1,512,2048]{2,1,0:T(8,128)(2,1)S(1)}, bf16[1,512,2048]{2,1,0:T(8,128)(2,1)}, u32[]{:S(2)}) copy-start(bf16[1,512,2048]{2,1,0:T(8,128)(2,1)} %param.7) | copy-start | bytes 6291460
Sparse Core Ops, SparseCore 0:
  301.3 52.7 all-reduce.1
